TPU v7x, 256 devices: a whole 4x4x8 slice. The times are simulated.
256 devices in a mesh: ctx: 64 (over z, x, core), head: 4 (over y).
Axes of the slice: x: 4, y: 4, z: 8, core: 2. Of those that a mesh axis runs over, the one named last changes fastest.
Arguments:
- mixer_input: bfloat16 [2, 4096, 16384], P(None, ('ctx', 'head')), may hold values from -6 to 6
- gate_input: bfloat16 [2, 4096, 16384], P(None, ('ctx', 'head')), may hold values from -6 to 6
- step_input: bfloat16 [2, 4096, 16384], P(None, ('ctx', 'head'))
- state_proj: bfloat16 [2, 4096, 32], P(None, 'ctx'), may hold values from -4 to 4
- conv_weight: bfloat16 [4, 16384], replicated, may hold values from -3 to 3
- conv_bias: float32 [16384], replicated, may hold values from -1 to 1
- step_bias: float32 [16384], P('head')
- decay_log: float32 [16, 16384], P(None, 'head'), may hold values from -0.7 to 0.7
- skip_gain: float32 [16384], P('head'), may hold values from 0.5 to 1.5
- query_states: bfloat16 [2, 4096, 8192], P(None, ('ctx', 'head')), may hold values from -5 to 5
- key_states: bfloat16 [2, 4096, 1024], P(None, ('ctx', 'head')), may hold values from -5 to 5
- value_states: bfloat16 [2, 4096, 1024], P(None, ('ctx', 'head')), may hold values from -6 to 6
- lengths: int32 [2], replicated, may hold values from 1024 to 4096, as said below
Outputs:
- mixer_output: bfloat16 [2, 4096, 16384], P(None, 'ctx', 'head')
- attention_output: bfloat16 [2, 4096, 8192], P(None, 'ctx', 'head')
Inputs may be any that keep to these rules, and one draw needn't show every extreme that they name: `lengths`: one of the 2 sequences has length 4096.
All inputs are finite; a program needn't handle non-finite values.
Results may differ from a plain program's by a relative error of at most 0.0043.
Values may be sent and summed in bfloat16 or wider, within the bound.
No kernel may reach another device: no remote copies, remote signals or barrier semaphores. Data moves between devices by JAX's collectives and lax.ppermute only.
A program may use at most 256 MiB of HBM per device.

v0:
```python
import math
import jax
import jax.numpy as jnp
from jax import lax
from jax.sharding import PartitionSpec as P

HD = 128
neg_large = -1e30


def passed_along(block, axis, distance):
    devices = range(lax.axis_size(axis))
    route = [(i - distance, i) for i in devices if i - distance in devices]
    return lax.ppermute(block, axis, route)


def carried_in(value, axis, join, neutral):
    count, mine = (lax.axis_size(axis), lax.axis_index(axis))
    pieces = jax.tree.map(lambda part: lax.all_gather(part, axis), value)
    total = jax.tree.map(
        lambda part, zero: jnp.full_like(part, 0) + jnp.asarray(zero, part.dtype), value, neutral
    )

    def step(position, total):
        longer = join(total, jax.tree.map(lambda part: part[position], pieces))
        return jax.tree.map(lambda new, old: jnp.where(position < mine, new, old), longer, total)

    return lax.fori_loop(0, count - 1, step, total)


def conv_rows(padded, conv_weight, conv_bias, row_count):
    running = (
        jnp.zeros((padded.shape[0], row_count, padded.shape[2]), jnp.float32)
        + conv_bias[None, None, :]
    )
    for tap_index in range(conv_weight.shape[0]):
        window = padded[:, tap_index : tap_index + row_count, :].astype(jnp.float32)
        running = running + window * conv_weight[tap_index].astype(jnp.float32)[None, None, :]
    return jax.nn.silu(running).astype(jnp.bfloat16)


def block_width(key_count):
    chosen = min(key_count, 512)
    while key_count % chosen != 0:
        chosen = chosen - 1
    return chosen


def empty_state(query_block):
    state_shape = (
        query_block.shape[0],
        query_block.shape[2],
        query_block.shape[3],
        query_block.shape[1],
    )
    return (
        jnp.full(state_shape, neg_large, jnp.float32),
        jnp.zeros(state_shape, jnp.float32),
        jnp.zeros(state_shape + (query_block.shape[4],), jnp.float32),
    )


def attend_block(
    carried, query_block, query_offset, key_block, value_block, key_offset, logit_scale_factor
):
    query_count = query_block.shape[1]
    key_count = key_block.shape[1]

    def compute(previous):
        row_peak, softmax_divisor, accumulated = previous
        score_matrix = (
            jnp.einsum(
                "brkgd,bskd->bkgrs", query_block, key_block, preferred_element_type=jnp.float32
            )
            * logit_scale_factor
        )
        query_pos = query_offset + jnp.arange(query_count, dtype=jnp.int32)
        key_pos = key_offset + jnp.arange(key_count, dtype=jnp.int32)
        allowed = key_pos[None, :] <= query_pos[:, None]
        score_matrix = jnp.where(allowed, score_matrix, neg_large)
        new_peak = jnp.maximum(row_peak, jnp.max(score_matrix, axis=-1))
        weights = jnp.where(allowed, jnp.exp(score_matrix - new_peak[..., None]), 0.0)
        fade_factor = jnp.exp(row_peak - new_peak)
        softmax_divisor = softmax_divisor * fade_factor + jnp.sum(weights, axis=-1)
        update = jnp.einsum(
            "bkgrs,bskd->bkgrd",
            weights.astype(jnp.bfloat16),
            value_block,
            preferred_element_type=jnp.float32,
        )
        accumulated = accumulated * fade_factor[..., None] + update
        return (new_peak, softmax_divisor, accumulated)

    def unchanged(previous):
        return previous

    return lax.cond(key_offset > query_offset + query_count - 1, unchanged, compute, carried)


def finish_rows(state_one):
    row_peak, softmax_divisor, accumulated = state_one
    normalised = accumulated / softmax_divisor[..., None]
    ordered = jnp.transpose(normalised, (0, 3, 1, 2, 4))
    return ordered.reshape(ordered.shape[0], ordered.shape[1], -1).astype(jnp.bfloat16)


def combine_carry(earlier, latter):
    return (earlier[0] * latter[0], latter[0] * earlier[1] + latter[1])


def shards(
    mixer_input,
    gate_input,
    step_input,
    state_proj,
    conv_weight,
    conv_bias,
    step_bias,
    decay_log,
    skip_gain,
    query_states,
    key_states,
    value_states,
    lengths,
):
    tap_count = conv_weight.shape[0]
    exchanged = (
        lax.all_to_all(mixer_input, "head", split_axis=2, concat_axis=1, tiled=True),
        lax.all_to_all(gate_input, "head", split_axis=2, concat_axis=1, tiled=True),
        lax.all_to_all(step_input, "head", split_axis=2, concat_axis=1, tiled=True),
        lax.all_to_all(query_states, "head", split_axis=2, concat_axis=1, tiled=True),
        lax.all_to_all(key_states, "head", split_axis=2, concat_axis=1, tiled=True),
        lax.all_to_all(value_states, "head", split_axis=2, concat_axis=1, tiled=True),
    )
    lead_local, gate_local, step_local, query_local, key_local, value_local = exchanged
    batch_size, row_count, channel_count = gate_local.shape
    channel_start = lax.axis_index("head") * channel_count
    weight_local = lax.dynamic_slice_in_dim(conv_weight, channel_start, channel_count, 1)
    bias_local = lax.dynamic_slice_in_dim(conv_bias, channel_start, channel_count, 0)
    tail_rows = lead_local[:, row_count - (tap_count - 1) :, :]
    before = passed_along(tail_rows, "ctx", 1)
    padded = jnp.concatenate([before, lead_local], axis=1)
    conv_out = conv_rows(padded, weight_local, bias_local, row_count)
    ctx_index = lax.axis_index("ctx")
    positions = ctx_index * row_count + jnp.arange(row_count, dtype=jnp.int32)
    live_rows = positions[None, :] < lengths[:, None]
    decay_rate = jnp.exp(decay_log)
    state_count = state_proj.shape[2] // 2
    conv_time = jnp.swapaxes(conv_out, 0, 1)
    step_time = jnp.swapaxes(step_local, 0, 1)
    proj_time = jnp.swapaxes(state_proj, 0, 1).astype(jnp.float32)
    readout_time = proj_time[:, :, state_count:]

    def advance(carry, inputs):
        state_now, elapsed_now = carry
        conv_row, step_row, proj_row = inputs
        step_row = jax.nn.softplus(step_row.astype(jnp.float32) + step_bias[None, :])
        elapsed_now = elapsed_now + step_row
        decay_now = jnp.exp(-step_row[:, None, :] * decay_rate[None])
        state_now = (
            decay_now * state_now
            + (step_row * conv_row.astype(jnp.float32))[:, None, :]
            * proj_row[:, :state_count, None]
        )
        return (
            (state_now, elapsed_now),
            (jnp.sum(proj_row[:, state_count:, None] * state_now, axis=1), elapsed_now),
        )

    start_state = jnp.zeros((batch_size, state_count, channel_count), jnp.float32)
    start_elapsed = jnp.zeros((batch_size, channel_count), jnp.float32)
    final_carry, scanned = lax.scan(
        advance, (start_state, start_elapsed), (conv_time, step_time, proj_time), unroll=8
    )
    final_state, total_elapsed = final_carry
    local_time, elapsed_time = scanned
    through = jnp.exp(-total_elapsed[:, None, :] * decay_rate[None])
    identity = (jnp.ones_like(through), jnp.zeros_like(final_state))
    prefix = carried_in((through, final_state), "ctx", combine_carry, identity)
    entering = prefix[1]
    carried = jnp.sum(
        readout_time[:, :, :, None]
        * jnp.exp(-elapsed_time[:, :, None, :] * decay_rate[None, None])
        * entering[None],
        axis=2,
    )
    mixed_time = (
        local_time + carried + skip_gain[None, None, :] * conv_time.astype(jnp.float32)
    ) * jax.nn.silu(jnp.swapaxes(gate_local, 0, 1).astype(jnp.float32))
    mixed_rows = jnp.swapaxes(mixed_time.astype(jnp.bfloat16), 0, 1)
    mixer_output = jnp.where(live_rows[:, :, None], mixed_rows, jnp.zeros((), jnp.bfloat16))
    kv_count = key_local.shape[2] // HD
    group_size = query_local.shape[2] // HD // kv_count
    query_five = query_local.reshape(batch_size, row_count, kv_count, group_size, HD)
    key_four = key_local.reshape(batch_size, row_count, kv_count, HD)
    value_four = value_local.reshape(batch_size, row_count, kv_count, HD)
    own_offset = ctx_index * row_count
    query_groups = [(query_five, own_offset)]
    logit_scale_factor = 1.0 / math.sqrt(HD)
    key_whole, value_whole = (
        lax.all_gather(key_four, "ctx", axis=1, tiled=True),
        lax.all_gather(value_four, "ctx", axis=1, tiled=True),
    )
    total_rows = key_whole.shape[1]
    chosen = block_width(total_rows)

    def one_block(block_index, current):
        key_block = lax.dynamic_slice_in_dim(key_whole, block_index * chosen, chosen, 1)
        value_block = lax.dynamic_slice_in_dim(value_whole, block_index * chosen, chosen, 1)
        key_offset = block_index * chosen
        return tuple(
            (
                attend_block(
                    state_one,
                    group[0],
                    group[1],
                    key_block,
                    value_block,
                    key_offset,
                    logit_scale_factor,
                )
                for state_one, group in zip(current, query_groups)
            )
        )

    initial = tuple((empty_state(group[0]) for group in query_groups))
    finished = lax.fori_loop(0, total_rows // chosen, one_block, initial)
    attended = finish_rows(finished[0])
    attention_output = jnp.where(live_rows[:, :, None], attended, jnp.zeros((), jnp.bfloat16))
    return (mixer_output, attention_output)


def solution(mesh):
    in_specs = (
        P(None, ("ctx", "head"), None),
        P(None, ("ctx", "head"), None),
        P(None, ("ctx", "head"), None),
        P(None, "ctx", None),
        P(),
        P(),
        P("head"),
        P(None, "head"),
        P("head"),
        P(None, ("ctx", "head"), None),
        P(None, ("ctx", "head"), None),
        P(None, ("ctx", "head"), None),
        P(),
    )
    out_specs = (P(None, "ctx", "head"), P(None, "ctx", "head"))
    return jax.shard_map(shards, mesh=mesh, in_specs=in_specs, out_specs=out_specs, check_vma=False)
```

profile of v0, /device:TPU:1, one launch (start us, length us, event | category | flops | bytes accessed | tf_op | source)
XLA Modules:
  0.0 620.2 jit_solution(5746733392723472344)
XLA Ops:
  9.0 9.3 %all_to_all.90 = bf16[4,2,4096]{2,1,0:T(2,128)(2,1)S(1)} all-to-all(bf16[4,2,4096]{2,1,0:T(2,128)(2,1)S(1)} %reshape.624), channel_id=1, replica_groups=mesh['ctx'=64,'head'=4] {'head'}, dimensions={0} | all-to-all | bytes 131072 | tf_op jit(solution)/shard_map/all_to_all | solution.py:132
  21.2 3.3 all-to-all-start.5
  24.5 12.7 %copy.123 = bf16[2,16,16384]{1,0,2:T(2,128)(2,1)} copy(bf16[2,16,16384]{2,1,0:T(8,128)(2,1)S(1)} %copy-done.6) | data formatting | bytes 2097152 | tf_op args[0]
  37.3 10.9 %reshape.620 = bf16[4,2,65536]{2,1,0:T(2,128)(2,1)} reshape(bf16[16384,2,16]{2,1,0:T(2,128)(2,1)} %bitcast.310) | data formatting | bytes 2097152
  48.2 4.3 all-to-all-start.1
  52.5 12.7 %copy.120 = bf16[2,16,16384]{1,0,2:T(2,128)(2,1)} copy(bf16[2,16,16384]{2,1,0:T(8,128)(2,1)S(1)} %copy-done.7) | data formatting | bytes 2097152 | tf_op args[2]
  65.2 10.9 %reshape.622 = bf16[4,2,65536]{2,1,0:T(2,128)(2,1)} reshape(bf16[16384,2,16]{2,1,0:T(2,128)(2,1)} %bitcast.311) | data formatting | bytes 2097152
  76.1 4.4 all-to-all-start
  81.2 7.2 %reshape.621 = bf16[16384,2,16]{2,1,0:T(2,128)(2,1)} reshape(bf16[4,2,65536]{2,1,0:T(2,128)(2,1)S(1)} %all-to-all-done.1) | data formatting | bytes 2097152
  88.4 16.6 %copy.124 = bf16[2,16,4,4096]{3,1,2,0:T(8,128)(2,1)S(1)} copy(bf16[2,16,4,4096]{1,0,3,2:T(2,128)(2,1)} %bitcast.308) | data formatting | bytes 2097152 | tf_op jit(solution)/shard_map/all_to_all | solution.py:128
  105.7 6.2 %collective-permute-start = (bf16[2,3,4096]{2,1,0:T(4,128)(2,1)}, bf16[2,3,4096]{2,1,0:T(4,128)(2,1)}, u32[]{:S(2)}, u32[]{:S(2)}) collective-permute-start(bf16[2,3,4096]{2,1,0:T(4,128)(2,1)} %slice.220), channel_id=1, source_target_pairs={{0,4},{4,8},{8,12},{12,16},{16,20},{20,24},{24,28},{28,32},{32,36}... | collective-permute-start | bytes 147464 | tf_op jit(solution)/shard_map/ppermute | solution.py:14
  114.4 7.2 %reshape.623 = bf16[16384,2,16]{2,1,0:T(2,128)(2,1)} reshape(bf16[4,2,65536]{2,1,0:T(2,128)(2,1)S(1)} %all-to-all-done) | data formatting | bytes 2097152
  121.6 19.1 %copy.145 = bf16[2,16,4,4096]{3,2,1,0:T(4,128)(2,1)S(1)} copy(bf16[2,16,4,4096]{1,0,3,2:T(2,128)(2,1)} %bitcast.309) | data formatting | bytes 2097152 | tf_op jit(solution)/shard_map/all_to_all | solution.py:130
  142.0 2.5 multiply_convert_fusion
  144.5 58.9 %while.51 = (s32[]{:T(128)}, f32[2,16,4096]{2,1,0:T(8,128)S(1)}, f32[2,4096]{1,0:T(2,128)S(1)}, f32[8,8,2,4096]{3,1,0,2:T(8,128)}, f32[8,8,2,4096]{3,2,1,0:T(2,1...) while((s32[]{:T(128)}, f32[2,16,4096]{2,1,0:T(8,128)S(1)}, ...), condition=%wide.region_9.10_spmd.clone, body=%wide.region_0.9_spmd.clone.sunk | while | flops 10469385 | bytes 9039950 | solution.py:172
  204.9 6.7 %copy.135 = bf16[2,16,8192]{1,0,2:T(2,128)(2,1)} copy(bf16[2,16,8192]{2,1,0:T(8,128)(2,1)S(1)} %copy-done.9) | data formatting | bytes 1048576 | tf_op args[9]
  211.6 6.5 %reshape.626 = bf16[4,2,32768]{2,1,0:T(2,128)(2,1)} reshape(bf16[8192,2,16]{2,1,0:T(2,128)(2,1)} %bitcast.314) | data formatting | bytes 1048576
  218.2 4.5 all-to-all-start.4
  222.7 12.7 %copy.131 = bf16[2,16,16384]{1,0,2:T(2,128)(2,1)} copy(bf16[2,16,16384]{2,1,0:T(8,128)(2,1)S(1)} %copy-done.8) | data formatting | bytes 2097152 | tf_op args[1]
  235.3 10.9 %reshape.618 = bf16[4,2,65536]{2,1,0:T(2,128)(2,1)} reshape(bf16[16384,2,16]{2,1,0:T(2,128)(2,1)} %bitcast.312) | data formatting | bytes 2097152
  246.3 4.4 all-to-all-start.2
  250.8 4.1 reshape.627
  254.9 9.1 %copy.136 = bf16[2,16,4,2048]{3,1,2,0:T(8,128)(2,1)S(1)} copy(bf16[2,16,4,2048]{1,0,3,2:T(2,128)(2,1)} %bitcast.313) | data formatting | bytes 1048576 | tf_op jit(solution)/shard_map/all_to_all | solution.py:131
  264.3 1.9 all-to-all-done.2
  266.1 7.1 %reshape.619 = bf16[16384,2,16]{2,1,0:T(2,128)(2,1)} reshape(bf16[4,2,65536]{2,1,0:T(2,128)(2,1)S(1)} %all-to-all-done.2) | data formatting | bytes 2097152
  273.2 18.8 %copy.132 = f32[2,16,4,4096]{3,1,2,0:T(8,128)} copy(bf16[2,16,4,4096]{1,0,3,2:T(2,128)(2,1)} %bitcast.307) | data formatting | bytes 3145728 | tf_op jit(solution)/shard_map/convert_element_type | solution.py:189
  292.1 4.9 neg.169
  296.9 5.0 copy.139
  301.9 4.7 copy.141
  306.7 6.5 %while.50 = (s32[]{:T(128)}, f32[2,2,8,64]{3,2,1,0:T(8,128)S(1)}, f32[2,2,8,64]{3,2,1,0:T(8,128)S(1)}, f32[2,2,8,64,128]{4,3,2,1,0:T(8,128)S(1)}, s32[]{:T(128)}...) while((s32[]{:T(128)}, f32[2,2,8,64]{3,2,1,0:T(8,128)S(1)}, ...), condition=%wide.region_18.19_spmd, body=%wide.region_13.18_spmd.sunk | while | flops 551064128 | bytes 16519977 | solution.py:227
  306.7 6.0 conditional.2
  306.8 1.8 fusion
  310.1 2.6 fusion.6
  315.0 34.7 %all-gather.6.cloned.1.call-done = f32[64,2,16,4096]{3,2,1,0:T(8,128)} async-done(((f32[1,2,16,4096]{3,2,1,0:T(8,128)}), f32[64,2,16,4096]{3,2,1,0:T(8,128)}) %all-gather.6.cloned.1.call-update) | async-done | bytes 33554448 | tf_op jit(solution)/shard_map/all_gather | solution.py:19
  349.7 142.1 %all-gather.12.cloned.1.call-done = f32[128,16,4096]{2,1,0:T(8,128)} async-done(((f32[2,16,4096]{2,1,0:T(8,128)}), f32[128,16,4096]{2,1,0:T(8,128)}) %all-gather.12.cloned.1.call-update) | async-done | bytes 33554448 | tf_op jit(solution)/shard_map/all_gather | solution.py:19
  491.9 105.7 %while.52 = (s32[]{:T(128)}, f32[2,16,4096]{2,1,0:T(8,128)S(1)}, s32[]{:T(128)}, f32[64,2,16,4096]{3,2,1,0:T(8,128)}, f32[64,2,16,4096]{3,2,1,0:T(8,128)}, /*index=5*/s32[]{:T(128)}, s32[]{:T(128)}) while((s32[]{:T(128)}, f32[2,16,4096]{2,1,0:T(8,128)S(1)}, s32[]{:T(128)}, f32[64,2,16,4096]{3,2,1,0:T(8,128)}, ...), condition=%wide.region_11.12_spmd.clone, body=%wide.region_10.11_spmd.clone.sunk | while | flops 524292 | bytes 2097253 | solution.py:28
  493.5 1.7 fusion.132
  495.2 1.7 fusion.132
  496.9 1.7 fusion.132
  498.6 1.7 fusion.132
  500.2 1.7 fusion.132
  503.6 1.7 fusion.132
  505.3 1.7 fusion.132
  507.0 1.7 fusion.132
  510.3 1.7 fusion.132
  512.0 1.7 fusion.132
  597.6 13.4 %multiply_reduce_fusion.8 = f32[64,2,4096]{2,1,0:T(2,128)S(1)} fusion(f32[2,16,4096]{2,1,0:T(8,128)S(1)} %get-tuple-element.472, f32[16,4096]{1,0:T(8,128)S(1)} %get-tuple-element.1256, f32[64,2,4096]{2,1,0:T(2,128)} %bitcast.327, f32[64,2,16]{2,1,0:T(2,128)S(1)} %copy.129), kind=kLoop, calls=%fused_computation.186 | loop fusion | flops 33030144 | bytes 4988928 | tf_op jit(solution)/shard_map/reduce_sum | solution.py:181
  611.0 2.7 bitcast_select_fusion.1
  (452 shorter events, 161.0 us)
Async XLA Ops:
  7.2 12.5 %copy-start.14 = (bf16[2,16,1024]{2,1,0:T(8,128)(2,1)S(1)}, bf16[2,16,1024]{2,1,0:T(8,128)(2,1)}, u32[]{:S(2)}) copy-start(bf16[2,16,1024]{2,1,0:T(8,128)(2,1)} %param.32) | copy-start | bytes 196612
  7.2 17.4 %copy-start.6 = (bf16[2,16,16384]{2,1,0:T(8,128)(2,1)S(1)}, bf16[2,16,16384]{2,1,0:T(8,128)(2,1)}, u32[]{:S(2)}) copy-start(bf16[2,16,16384]{2,1,0:T(8,128)(2,1)} %param.21) | copy-start | bytes 3145732
  7.2 289.7 %all-gather.8.cloned.1.call-start = ((), (), s32[]{:S(2)}) async-start(), calls=%async_computation.7 | async-start | bytes 4259840 | tf_op jit(solution)/shard_map/all_gather | solution.py:201
  21.2 27.0 %all-to-all-start.5 = ((bf16[4,2,4096]{2,1,0:T(2,128)(2,1)}), bf16[4,2,4096]{2,1,0:T(2,128)(2,1)S(1)}, u32[]{:S(2)}, u32[]{:S(2)}) async-start(bf16[4,2,4096]{2,1,0:T(2,128)(2,1)} %reshape.628), calls=%async_computation.5 | async-start | bytes 131072 | tf_op jit(solution)/shard_map/all_to_all | solution.py:133
  48.2 4.3 copy-start.7
  48.2 27.9 %all-to-all-start.1 = ((bf16[4,2,65536]{2,1,0:T(2,128)(2,1)}), bf16[4,2,65536]{2,1,0:T(2,128)(2,1)S(1)}, u32[]{:S(2)}, u32[]{:S(2)}) async-start(bf16[4,2,65536]{2,1,0:T(2,128)(2,1)} %reshape.620), calls=%async_computation.1 | async-start | bytes 2097152 | tf_op jit(solution)/shard_map/all_to_all | solution.py:128
  76.1 4.4 copy-start.15
  76.1 38.3 %all-to-all-start = ((bf16[4,2,65536]{2,1,0:T(2,128)(2,1)}), bf16[4,2,65536]{2,1,0:T(2,128)(2,1)S(1)}, u32[]{:S(2)}, u32[]{:S(2)}) async-start(bf16[4,2,65536]{2,1,0:T(2,128)(2,1)} %reshape.622), calls=%async_computation | async-start | bytes 2097152 | tf_op jit(solution)/shard_map/all_to_all | solution.py:130
  80.5 221.4 %all-gather.10.cloned.1.call-start = ((), (), s32[]{:S(2)}) async-start(), calls=%async_computation.8 | async-start | bytes 4259840 | tf_op jit(solution)/shard_map/all_gather | solution.py:202
  88.4 23.6 %copy-start.17 = (bf16[2,64,32]{1,2,0:T(8,128)(2,1)S(1)}, bf16[2,64,32]{1,2,0:T(8,128)(2,1)}, u32[]{:S(2)}) copy-start(bf16[2,64,32]{1,2,0:T(8,128)(2,1)} %param.24) | copy-start | bytes 24580
  88.4 23.6 %copy-start.10 = (f32[16,4096]{1,0:T(8,128)S(1)}, f32[16,4096]{1,0:T(8,128)}, u32[]{:S(2)}) copy-start(f32[16,4096]{1,0:T(8,128)} %param.28) | copy-start | bytes 786436
  105.0 16.6 %copy-start.3 = (bf16[2,16,4,4096]{3,1,2,0:T(8,128)(2,1)}, bf16[2,16,4,4096]{3,1,2,0:T(8,128)(2,1)S(1)}, u32[]{:S(2)}) copy-start(bf16[2,16,4,4096]{3,1,2,0:T(8,128)(2,1)S(1)} %copy.124) | copy-start | bytes 3145732
  105.7 35.7 %collective-permute-start = (bf16[2,3,4096]{2,1,0:T(4,128)(2,1)}, bf16[2,3,4096]{2,1,0:T(4,128)(2,1)}, u32[]{:S(2)}, u32[]{:S(2)}) collective-permute-start(bf16[2,3,4096]{2,1,0:T(4,128)(2,1)} %slice.220), channel_id=1, source_target_pairs={{0,4},{4,8},{8,12},{12,16},{16,20},{20,24},{24,28},{28,32},{32,36}... | collective-permute-start | bytes 147464 | tf_op jit(solution)/shard_map/ppermute | solution.py:14
  114.2 235.5 %all-gather.6.cloned.1.call-start = ((), (), s32[]{:S(2)}) async-start(), calls=%async_computation.6 | async-start | bytes 34078720 | tf_op jit(solution)/shard_map/all_gather | solution.py:19
  140.8 1.2 copy-start.4
  140.8 1.2 dynamic-slice-start
  140.8 1.2 copy-start.11
  140.8 1.2 copy-start.12
  140.8 1.2 copy-start.13
  140.8 3.7 copy-start.1
  203.4 1.0 copy-start
  203.4 1.5 copy-start.9
  204.4 287.5 %all-gather.12.cloned.1.call-start = ((), (), s32[]{:S(2)}) async-start(), calls=%async_computation.9 | async-start | bytes 34078720 | tf_op jit(solution)/shard_map/all_gather | solution.py:19
  211.6 11.0 %copy-start.8 = (bf16[2,16,16384]{2,1,0:T(8,128)(2,1)S(1)}, bf16[2,16,16384]{2,1,0:T(8,128)(2,1)}, u32[]{:S(2)}) copy-start(bf16[2,16,16384]{2,1,0:T(8,128)(2,1)} %param.22) | copy-start | bytes 3145732
  218.2 28.1 %all-to-all-start.4 = ((bf16[4,2,32768]{2,1,0:T(2,128)(2,1)}), bf16[4,2,32768]{2,1,0:T(2,128)(2,1)S(1)}, u32[]{:S(2)}, u32[]{:S(2)}) async-start(bf16[4,2,32768]{2,1,0:T(2,128)(2,1)} %reshape.626), calls=%async_computation.4 | async-start | bytes 1048576 | tf_op jit(solution)/shard_map/all_to_all | solution.py:131
  246.3 4.5 copy-start.18
  246.3 19.9 %all-to-all-start.2 = ((bf16[4,2,65536]{2,1,0:T(2,128)(2,1)}), bf16[4,2,65536]{2,1,0:T(2,128)(2,1)S(1)}, u32[]{:S(2)}, u32[]{:S(2)}) async-start(bf16[4,2,65536]{2,1,0:T(2,128)(2,1)} %reshape.618), calls=%async_computation.2 | async-start | bytes 2097152 | tf_op jit(solution)/shard_map/all_to_all | solution.py:129
  597.6 13.4 %copy-start.2 = (f32[2,16,4,4096]{3,1,2,0:T(8,128)S(1)}, f32[2,16,4,4096]{3,1,2,0:T(8,128)}, u32[]{:S(2)}) copy-start(f32[2,16,4,4096]{3,1,2,0:T(8,128)} %copy.132) | copy-start | bytes 6291460
  597.6 13.4 %copy-start.5 = (f32[8,8,2,4096]{3,1,0,2:T(8,128)S(1)}, f32[8,8,2,4096]{3,1,0,2:T(8,128)}, u32[]{:S(2)}) copy-start(f32[8,8,2,4096]{3,1,0,2:T(8,128)} %get-tuple-element.468) | copy-start | bytes 6291460
  597.6 13.4 %copy-start.16 = (f32[4096]{0:T(1024)S(1)}, f32[4096]{0:T(1024)}, u32[]{:S(2)}) copy-start(f32[4096]{0:T(1024)} %param.29) | copy-start | bytes 49156
Sparse Core Ops, SparseCore 0:
  19.8 81.7 all-gather.7
  114.3 81.8 all-gather.9
  204.5 145.1 all-gather.5
  352.3 139.4 all-gather.11
where the time goes:
time: 625 us; the launch traced here: 620 us
  local copies, waits for them, and re-layouts  220 us (35%)
  waiting for transfers between devices  179 us (29%)
  other arithmetic  163 us (26%)
  starting transfers between devices  27.3 us (4%)
  between operations  14.2 us (2%)
  blocking collectives  9.29 us (1%)
    all_gather x2, waiting for transfers between devices, carried_in(): pieces = jax.tree.map(lambda part: lax.all_gather(part, axis), value)  177 us
    unnamed x57, local copies, waits for them, and re-layouts  114 us
    select_n x63, other arithmetic, step(): jnp.where(position < mine, new, old)  104 us
    reduce_sum x24, other arithmetic, advance(): jnp.sum(proj_row[:, state_count:, None] * state_now, axis=1)  20.5 us
    all_to_all x2, local copies, waits for them, and re-layouts, shards(): lax.all_to_all(step_input, 'head', split_axis=2, concat_axis=1, tiled=True)  19.7 us
    convert_element_type x1, local copies, waits for them, and re-layouts, shards(): jnp.swapaxes(gate_local, 0, 1).astype(jnp.float32)  18.8 us
    all_to_all x1, local copies, waits for them, and re-layouts, shards(): lax.all_to_all(mixer_input, 'head', split_axis=2, concat_axis=1, tiled=True)  16.6 us
    reduce_sum x1, other arithmetic, shards(): jnp.sum(readout_time[:, :, :, None] * jnp.exp(-elapsed_time[:, :, None, :...  13.4 us
  transfers between devices with their start and end apart: 10, of which 3 were waited for; matrix products, arithmetic and copies ran while one was open for 42% of the time, Pallas kernels for 0%

commit v1 on v0

--- a/solution.py
+++ b/solution.py
@@ -1,3 +1,4 @@
+import functools
 import math
 import jax
 import jax.numpy as jnp
@@ -6,6 +7,28 @@
 
 HD = 128
 neg_large = -1e30
+
+
+def attach_state(u_in, named_axis):
+    opened, kept_arr = (lax.axis_size(named_axis), lax.axis_index(named_axis))
+    next_value = u_in.shape[2] // opened
+    z_new = list(u_in.shape)
+    z_new[2] = next_value
+    tile_out = z_new[1]
+    z_new[1] = tile_out * opened
+    res = jnp.zeros(z_new, u_in.dtype)
+    for k in range(opened):
+        local_next = lax.dynamic_slice_in_dim(u_in, (kept_arr ^ k) * next_value, next_value, axis=2)
+        if k:
+            entries = []
+            for h in range(opened):
+                entries.append((h, h ^ k))
+            local_next = lax.ppermute(local_next, axis_name=named_axis, perm=entries)
+        res = lax.dynamic_update_slice_in_dim(res, local_next, (kept_arr ^ k) * tile_out, axis=1)
+    return res
+
+
+process_the_slot = functools.partial(attach_state, named_axis="head")
 
 
 def passed_along(block, axis, distance):
@@ -125,7 +148,7 @@
 ):
     tap_count = conv_weight.shape[0]
     exchanged = (
-        lax.all_to_all(mixer_input, "head", split_axis=2, concat_axis=1, tiled=True),
+        process_the_slot(mixer_input),
         lax.all_to_all(gate_input, "head", split_axis=2, concat_axis=1, tiled=True),
         lax.all_to_all(step_input, "head", split_axis=2, concat_axis=1, tiled=True),
         lax.all_to_all(query_states, "head", split_axis=2, concat_axis=1, tiled=True),

time: 625 us -> 598 us (0.957)
  local copies, waits for them, and re-layouts: 220 us -> 179 us
  waiting for transfers between devices: 179 us -> 197 us
    unnamed x57 -> x44, local copies, waits for them, and re-layouts: 114 us -> 86.7 us
    all_to_all x1 -> x0, local copies, waits for them, and re-layouts: 16.6 us -> none  [shards(): lax.all_to_all(mixer_input, 'head', split_axis=2, concat_axis=1, tiled=True)]
    all_to_all x1, waiting for transfers between devices: 0.01 us -> 9.32 us  [shards(): lax.all_to_all(step_input, 'head', split_axis=2, concat_axis=1, tiled=True)]
  transfers between devices with their start and end apart: 10 -> 12, of which waited for: 3 -> 5; matrix products, arithmetic and copies ran while one was open for 42% -> 37% of each run, Pallas kernels for 0% -> 0%
where the time goes in v1:
time: 598 us; the launch traced here: 594 us
  waiting for transfers between devices  197 us (33%)
  local copies, waits for them, and re-layouts  179 us (30%)
  other arithmetic  162 us (27%)
  starting transfers between devices  25.4 us (4%)
  between operations  14.2 us (2%)
  blocking collectives  9.29 us (2%)
    all_gather x2, waiting for transfers between devices, carried_in(): pieces = jax.tree.map(lambda part: lax.all_gather(part, axis), value)  181 us
    select_n x63, other arithmetic, step(): jnp.where(position < mine, new, old)  104 us
    unnamed x44, local copies, waits for them, and re-layouts  86.7 us
    all_to_all x2, local copies, waits for them, and re-layouts, shards(): lax.all_to_all(step_input, 'head', split_axis=2, concat_axis=1, tiled=True)  21.9 us
    reduce_sum x24, other arithmetic, advance(): jnp.sum(proj_row[:, state_count:, None] * state_now, axis=1)  20.5 us
    convert_element_type x1, local copies, waits for them, and re-layouts, shards(): jnp.swapaxes(gate_local, 0, 1).astype(jnp.float32)  18.8 us
    reduce_sum x1, other arithmetic, shards(): jnp.sum(readout_time[:, :, :, None] * jnp.exp(-elapsed_time[:, :, None, :...  13.4 us
    dynamic_update_slice x16, local copies, waits for them, and re-layouts, shards(): lax.scan(advance, (start_state, start_elapsed), (conv_time, step_time, pr...  12.8 us
  transfers between devices with their start and end apart: 12, of which 5 were waited for; matrix products, arithmetic and copies ran while one was open for 37% of the time, Pallas kernels for 0%

profile of v1, /device:TPU:1, one launch (start us, length us, event | category | flops | bytes accessed | tf_op | source)
XLA Modules:
  0.0 593.7 jit_solution(15792474687400682048)
XLA Ops:
  9.0 9.3 %all_to_all.72 = bf16[4,2,4096]{2,1,0:T(2,128)(2,1)S(1)} all-to-all(bf16[4,2,4096]{2,1,0:T(2,128)(2,1)S(1)} %reshape.622), channel_id=1, replica_groups=mesh['ctx'=64,'head'=4] {'head'}, dimensions={0} | all-to-all | bytes 131072 | tf_op jit(solution)/shard_map/all_to_all | solution.py:155
  21.0 1.8 collective-permute-start.1
  22.8 1.8 collective-permute-start.2
  26.1 3.3 all-to-all-start.4
  29.4 1.7 dynamic-slice_convert_fusion.3
  31.1 1.7 collective-permute-done.1
  32.8 3.7 collective-permute-done.2
  36.6 5.5 collective-permute-start.3
  43.9 12.7 %copy.114 = bf16[2,16,16384]{1,0,2:T(2,128)(2,1)} copy(bf16[2,16,16384]{2,1,0:T(8,128)(2,1)S(1)} %copy-done.5) | data formatting | bytes 2097152 | tf_op args[2]
  56.6 10.9 %reshape.620 = bf16[4,2,65536]{2,1,0:T(2,128)(2,1)} reshape(bf16[16384,2,16]{2,1,0:T(2,128)(2,1)} %bitcast.303) | data formatting | bytes 2097152
  67.5 4.4 all-to-all-start
  74.2 2.5 multiply_convert_fusion
  76.8 9.3 %all-to-all-done = bf16[4,2,65536]{2,1,0:T(2,128)(2,1)} async-done(((bf16[4,2,65536]{2,1,0:T(2,128)(2,1)}), bf16[4,2,65536]{2,1,0:T(2,128)(2,1)}, u32[]{:S(2)}, u32[]{:S(2)}) %all-to-all-start) | async-done | bytes 1048608 | tf_op jit(solution)/shard_map/all_to_all | solution.py:153
  86.1 8.2 %reshape.621 = bf16[16384,2,16]{2,1,0:T(2,128)(2,1)} reshape(bf16[4,2,65536]{2,1,0:T(2,128)(2,1)} %all-to-all-done) | data formatting | bytes 2097152
  94.3 20.1 %copy.137 = bf16[2,16,4,4096]{3,2,1,0:T(4,128)(2,1)} copy(bf16[2,16,4,4096]{1,0,3,2:T(2,128)(2,1)} %bitcast.302) | data formatting | bytes 2097152 | tf_op jit(solution)/shard_map/all_to_all | solution.py:153
  114.4 1.8 copy.116
  116.2 59.0 %while.51 = (s32[]{:T(128)}, f32[2,16,4096]{2,1,0:T(8,128)S(1)}, f32[2,4096]{1,0:T(2,128)S(1)}, f32[8,8,2,4096]{3,1,0,2:T(8,128)}, f32[8,8,2,4096]{3,2,1,0:T(2,1...) while((s32[]{:T(128)}, f32[2,16,4096]{2,1,0:T(8,128)S(1)}, ...), condition=%wide.region_9.10_spmd.clone, body=%wide.region_0.9_spmd.clone.sunk | while | flops 10469385 | bytes 9039950 | solution.py:195
  176.8 6.7 %copy.127 = bf16[2,16,8192]{1,0,2:T(2,128)(2,1)} copy(bf16[2,16,8192]{2,1,0:T(8,128)(2,1)S(1)} %copy-done.8) | data formatting | bytes 1048576 | tf_op args[9]
  183.5 6.5 %reshape.624 = bf16[4,2,32768]{2,1,0:T(2,128)(2,1)} reshape(bf16[8192,2,16]{2,1,0:T(2,128)(2,1)} %bitcast.306) | data formatting | bytes 1048576
  190.0 3.5 all-to-all-start.3
  193.5 12.8 %copy.123 = bf16[2,16,16384]{1,0,2:T(2,128)(2,1)} copy(bf16[2,16,16384]{2,1,0:T(8,128)(2,1)S(1)} %copy-done.6) | data formatting | bytes 2097152 | tf_op args[1]
  206.3 11.0 %reshape.618 = bf16[4,2,65536]{2,1,0:T(2,128)(2,1)} reshape(bf16[16384,2,16]{2,1,0:T(2,128)(2,1)} %bitcast.304) | data formatting | bytes 2097152
  217.3 4.5 all-to-all-start.1
  222.0 4.1 reshape.625
  226.1 9.0 %copy.128 = bf16[2,16,4,2048]{3,1,2,0:T(8,128)(2,1)S(1)} copy(bf16[2,16,4,2048]{1,0,3,2:T(2,128)(2,1)} %bitcast.305) | data formatting | bytes 1048576 | tf_op jit(solution)/shard_map/all_to_all | solution.py:154
  235.4 1.8 copy-done.3
  237.2 2.5 neg.169
  239.7 7.1 %reshape.619 = bf16[16384,2,16]{2,1,0:T(2,128)(2,1)} reshape(bf16[4,2,65536]{2,1,0:T(2,128)(2,1)S(1)} %all-to-all-done.1) | data formatting | bytes 2097152
  246.8 18.8 %copy.124 = f32[2,16,4,4096]{3,1,2,0:T(8,128)} copy(bf16[2,16,4,4096]{1,0,3,2:T(2,128)(2,1)} %bitcast.301) | data formatting | bytes 3145728 | tf_op jit(solution)/shard_map/convert_element_type | solution.py:212
  265.5 4.9 copy.131
  270.5 5.0 copy.133
  275.6 6.5 %while.50 = (s32[]{:T(128)}, f32[2,2,8,64]{3,2,1,0:T(8,128)S(1)}, f32[2,2,8,64]{3,2,1,0:T(8,128)S(1)}, f32[2,2,8,64,128]{4,3,2,1,0:T(8,128)S(1)}, s32[]{:T(128)}...) while((s32[]{:T(128)}, f32[2,2,8,64]{3,2,1,0:T(8,128)S(1)}, ...), condition=%wide.region_18.19_spmd, body=%wide.region_13.18_spmd.sunk | while | flops 551064128 | bytes 16519977 | solution.py:250
  275.6 5.9 conditional.2
  275.7 1.8 fusion
  279.0 2.6 fusion.6
  283.9 39.4 %all-gather.6.cloned.1.call-done = f32[64,2,16,4096]{3,2,1,0:T(8,128)} async-done(((f32[1,2,16,4096]{3,2,1,0:T(8,128)}), f32[64,2,16,4096]{3,2,1,0:T(8,128)}) %all-gather.6.cloned.1.call-update) | async-done | bytes 33554448 | tf_op jit(solution)/shard_map/all_gather | solution.py:42
  323.3 142.1 %all-gather.12.cloned.1.call-done = f32[128,16,4096]{2,1,0:T(8,128)} async-done(((f32[2,16,4096]{2,1,0:T(8,128)}), f32[128,16,4096]{2,1,0:T(8,128)}) %all-gather.12.cloned.1.call-update) | async-done | bytes 33554448 | tf_op jit(solution)/shard_map/all_gather | solution.py:42
  465.4 105.7 %while.52 = (s32[]{:T(128)}, f32[2,16,4096]{2,1,0:T(8,128)S(1)}, s32[]{:T(128)}, f32[64,2,16,4096]{3,2,1,0:T(8,128)}, f32[64,2,16,4096]{3,2,1,0:T(8,128)}, /*index=5*/s32[]{:T(128)}, s32[]{:T(128)}) while((s32[]{:T(128)}, f32[2,16,4096]{2,1,0:T(8,128)S(1)}, s32[]{:T(128)}, f32[64,2,16,4096]{3,2,1,0:T(8,128)}, ...), condition=%wide.region_11.12_spmd.clone, body=%wide.region_10.11_spmd.clone.sunk | while | flops 524292 | bytes 2097253 | solution.py:51
  468.8 1.7 fusion.132
  470.4 1.7 fusion.132
  472.1 1.7 fusion.132
  473.8 1.7 fusion.132
  475.5 1.7 fusion.132
  477.1 1.7 fusion.132
  480.5 1.7 fusion.132
  482.2 1.7 fusion.132
  571.1 13.4 %multiply_reduce_fusion.8 = f32[64,2,4096]{2,1,0:T(2,128)S(1)} fusion(f32[2,16,4096]{2,1,0:T(8,128)S(1)} %get-tuple-element.472, f32[16,4096]{1,0:T(8,128)S(1)} %get-tuple-element.1260, f32[64,2,4096]{2,1,0:T(2,128)} %bitcast.317, f32[64,2,16]{2,1,0:T(2,128)S(1)} %copy.121), kind=kLoop, calls=%fused_computation.186 | loop fusion | flops 33030144 | bytes 4988928 | tf_op jit(solution)/shard_map/reduce_sum | solution.py:204
  584.5 2.7 bitcast_select_fusion.1
  (447 shorter events, 164.7 us)
Async XLA Ops:
  7.2 12.6 %copy-start.7 = (bf16[2,16,16384]{2,1,0:T(8,128)(2,1)S(1)}, bf16[2,16,16384]{2,1,0:T(8,128)(2,1)}, u32[]{:S(2)}) copy-start(bf16[2,16,16384]{2,1,0:T(8,128)(2,1)} %param.21) | copy-start | bytes 3145732
  7.2 258.4 %all-gather.8.cloned.1.call-start = ((), (), s32[]{:S(2)}) async-start(), calls=%async_computation.6 | async-start | bytes 4259840 | tf_op jit(solution)/shard_map/all_gather | solution.py:224
  18.6 5.9 copy-start.9
  20.7 21.4 %copy-start.12 = (bf16[2,64,32]{1,2,0:T(8,128)(2,1)S(1)}, bf16[2,64,32]{1,2,0:T(8,128)(2,1)}, u32[]{:S(2)}) copy-start(bf16[2,64,32]{1,2,0:T(8,128)(2,1)} %param.24) | copy-start | bytes 24580
  20.7 23.2 %copy-start.5 = (bf16[2,16,16384]{2,1,0:T(8,128)(2,1)S(1)}, bf16[2,16,16384]{2,1,0:T(8,128)(2,1)}, u32[]{:S(2)}) copy-start(bf16[2,16,16384]{2,1,0:T(8,128)(2,1)} %param.23) | copy-start | bytes 3145732
  20.7 10.4 %collective-permute-start = (bf16[2,16,4096]{2,1,0:T(8,128)(2,1)}, bf16[2,16,4096]{2,1,0:T(8,128)(2,1)S(1)}, u32[]{:S(2)}, u32[]{:S(2)}) collective-permute-start(bf16[2,16,4096]{2,1,0:T(8,128)(2,1)} %get-tuple-element.807), channel_id=1, source_target_pairs={{0,1},{1,0},{2,3},{3,2},{4,5},{5,4},{6,7},{7,6},{8,9},{9,8},{10,11... | collective-permute-start | bytes 786440 | tf_op jit(solution)/shard_map/ppermute | solution.py:26
  21.0 11.8 %collective-permute-start.1 = (bf16[2,16,4096]{2,1,0:T(8,128)(2,1)}, bf16[2,16,4096]{2,1,0:T(8,128)(2,1)S(1)}, u32[]{:S(2)}, u32[]{:S(2)}) collective-permute-start(bf16[2,16,4096]{2,1,0:T(8,128)(2,1)} %get-tuple-element.809), channel_id=1, source_target_pairs={{0,2},{1,3},{2,0},{3,1},{4,6},{5,7},{6,4},{7,5},{8,10},{9,11},{10,... | collective-permute-start | bytes 786440 | tf_op jit(solution)/shard_map/ppermute | solution.py:26
  22.8 13.8 %collective-permute-start.2 = (bf16[2,16,4096]{2,1,0:T(8,128)(2,1)}, bf16[2,16,4096]{2,1,0:T(8,128)(2,1)S(1)}, u32[]{:S(2)}, u32[]{:S(2)}) collective-permute-start(bf16[2,16,4096]{2,1,0:T(8,128)(2,1)} %get-tuple-element.806), channel_id=1, source_target_pairs={{0,3},{1,2},{2,1},{3,0},{4,7},{5,6},{6,5},{7,4},{8,11},{9,10},{10,... | collective-permute-start | bytes 786440 | tf_op jit(solution)/shard_map/ppermute | solution.py:26
  26.1 41.5 %all-to-all-start.4 = ((bf16[4,2,4096]{2,1,0:T(2,128)(2,1)}), bf16[4,2,4096]{2,1,0:T(2,128)(2,1)S(1)}, u32[]{:S(2)}, u32[]{:S(2)}) async-start(bf16[4,2,4096]{2,1,0:T(2,128)(2,1)} %reshape.626), calls=%async_computation.4 | async-start | bytes 131072 | tf_op jit(solution)/shard_map/all_to_all | solution.py:156
  36.6 37.0 %collective-permute-start.3 = (bf16[2,3,4096]{2,1,0:T(4,128)(2,1)S(1)}, bf16[2,3,4096]{2,1,0:T(4,128)(2,1)S(1)}, u32[]{:S(2)}, u32[]{:S(2)}) collective-permute-start(bf16[2,3,4096]{2,1,0:T(4,128)(2,1)S(1)} %slice.220), channel_id=1, source_target_pairs={{0,4},{4,8},{8,12},{12,16},{16,20},{20,24},{24,28},{28,32},{32,36}... | collective-permute-start | bytes 147464 | tf_op jit(solution)/shard_map/ppermute | solution.py:37
  67.5 6.7 %dynamic-slice-start = ((f32[16384]{0:T(1024)}, s32[]{:T(128)}), f32[4096]{0:T(1024)S(1)}, s32[]{:S(2)}) async-start(f32[16384]{0:T(1024)} %param.26, s32[]{:T(128)} %select_n.162), calls=%async_computation.9 | async-start | bytes 33280 | tf_op jit(solution)/shard_map/dynamic_slice | solution.py:162
  67.5 18.6 %all-to-all-start = ((bf16[4,2,65536]{2,1,0:T(2,128)(2,1)}), bf16[4,2,65536]{2,1,0:T(2,128)(2,1)}, u32[]{:S(2)}, u32[]{:S(2)}) async-start(bf16[4,2,65536]{2,1,0:T(2,128)(2,1)} %reshape.620), calls=%async_computation | async-start | bytes 2097152 | tf_op jit(solution)/shard_map/all_to_all | solution.py:153
  71.9 198.6 %all-gather.10.cloned.1.call-start = ((), (), s32[]{:S(2)}) async-start(), calls=%async_computation.7 | async-start | bytes 4259840 | tf_op jit(solution)/shard_map/all_gather | solution.py:225
  73.4 249.9 %all-gather.6.cloned.1.call-start = ((), (), s32[]{:S(2)}) async-start(), calls=%async_computation.5 | async-start | bytes 34078720 | tf_op jit(solution)/shard_map/all_gather | solution.py:42
  73.6 0.6 copy-start.10
  114.4 1.8 copy-start.1
  175.2 1.0 copy-start
  175.2 1.5 copy-start.8
  176.2 289.2 %all-gather.12.cloned.1.call-start = ((), (), s32[]{:S(2)}) async-start(), calls=%async_computation.8 | async-start | bytes 34078720 | tf_op jit(solution)/shard_map/all_gather | solution.py:42
  183.5 10.0 %copy-start.6 = (bf16[2,16,16384]{2,1,0:T(8,128)(2,1)S(1)}, bf16[2,16,16384]{2,1,0:T(8,128)(2,1)}, u32[]{:S(2)}) copy-start(bf16[2,16,16384]{2,1,0:T(8,128)(2,1)} %param.22) | copy-start | bytes 3145732
  190.0 27.3 %all-to-all-start.3 = ((bf16[4,2,32768]{2,1,0:T(2,128)(2,1)}), bf16[4,2,32768]{2,1,0:T(2,128)(2,1)S(1)}, u32[]{:S(2)}, u32[]{:S(2)}) async-start(bf16[4,2,32768]{2,1,0:T(2,128)(2,1)} %reshape.624), calls=%async_computation.3 | async-start | bytes 1048576 | tf_op jit(solution)/shard_map/all_to_all | solution.py:154
  217.3 4.6 copy-start.13
  217.3 22.4 %all-to-all-start.1 = ((bf16[4,2,65536]{2,1,0:T(2,128)(2,1)}), bf16[4,2,65536]{2,1,0:T(2,128)(2,1)S(1)}, u32[]{:S(2)}, u32[]{:S(2)}) async-start(bf16[4,2,65536]{2,1,0:T(2,128)(2,1)} %reshape.618), calls=%async_computation.1 | async-start | bytes 2097152 | tf_op jit(solution)/shard_map/all_to_all | solution.py:152
  235.1 2.1 copy-start.3
  571.1 13.4 %copy-start.2 = (f32[2,16,4,4096]{3,1,2,0:T(8,128)S(1)}, f32[2,16,4,4096]{3,1,2,0:T(8,128)}, u32[]{:S(2)}) copy-start(f32[2,16,4,4096]{3,1,2,0:T(8,128)} %copy.124) | copy-start | bytes 6291460
  571.1 13.4 %copy-start.4 = (f32[8,8,2,4096]{3,1,0,2:T(8,128)S(1)}, f32[8,8,2,4096]{3,1,0,2:T(8,128)}, u32[]{:S(2)}) copy-start(f32[8,8,2,4096]{3,1,0,2:T(8,128)} %get-tuple-element.468) | copy-start | bytes 6291460
  571.1 13.4 %copy-start.11 = (f32[4096]{0:T(1024)S(1)}, f32[4096]{0:T(1024)}, u32[]{:S(2)}) copy-start(f32[4096]{0:T(1024)} %param.29) | copy-start | bytes 49156
Sparse Core Ops, SparseCore 0:
  19.8 81.7 all-gather.7
  104.4 76.1 all-gather.9
  183.4 139.8 all-gather.5
  325.9 139.4 all-gather.11
